TPU v7x, 256 devices: a whole 4x4x8 slice. The times are simulated.
256 devices in a mesh: blk: 32 (over y, z), rep: 8 (over x, core).
Axes of the slice: x: 4, y: 4, z: 8, core: 2. Of those that a mesh axis runs over, the one named last changes fastest.
Arguments:
- hidden_in: bfloat16 [8, 512, 2560], P('rep', 'blk'), may hold values from -6 to 6
- w_z: bfloat16 [2560, 4096], P(None, 'blk'), may hold values from -0.125 to 0.125
- w_x: bfloat16 [2560, 4096], P(None, 'blk'), may hold values from -0.125 to 0.125
- w_bc: bfloat16 [2560, 256], replicated, may hold values from -0.125 to 0.125
- w_dt: bfloat16 [2560, 64], P(None, 'blk'), may hold values from -0.125 to 0.125
- conv_x: float32 [4, 4096], P(None, 'blk'), may hold values from -3 to 3
- conv_bc: float32 [4, 256], replicated, may hold values from -3 to 3
- dt_bias: float32 [4, 64], P(None, 'blk'), may hold values from -3 to -0.5
- a_log: float32 [64], P('blk'), may hold values from -2.5 to 0.5
- d_skip: float32 [64], P('blk'), may hold values from 0.5 to 1.5
- norm_gain: float32 [4096], P('blk'), may hold values from 0.5 to 1.5
- w_out: bfloat16 [4096, 2560], P('blk'), may hold values from -0.09375 to 0.09375
- edge_x: bfloat16 [256, 3, 4096], P('rep', None, 'blk'), may hold values from -6 to 6
- edge_bc: bfloat16 [256, 3, 256], P('rep'), may hold values from -6 to 6
- pool: float32 [384, 64, 64, 128], P('rep', 'blk'), may hold values from -0.6 to 0.6
- tenant_sizes: int32 [4], replicated, may hold values from 1 to 128, 256 in all
- owner: int32 [256, 1], P('rep'), may hold values from 0 to 7; in each aligned block of 32 rows (0 to 31, 32 to 63, ...) at most 6 rows name the same one
- accepted: int32 [256], P('rep'), may hold values from 1 to 16
- prompt_len: int32 [256], P('rep'), may hold values from 1 to 11
Outputs:
- hidden_out: bfloat16 [8, 512, 2560], P('rep', 'blk')
- new_pool: float32 [384, 64, 64, 128], P('rep', 'blk')
Inputs may be any that keep to these rules, and one draw needn't show every extreme that they name: Among the requests of one group (aligned blocks of 32 requests) each owner is named at most 6 times, a bound that some block reaches. `tenant_sizes`: the sizes sum to 256.
All inputs are finite; a program needn't handle non-finite values.
Results may differ from a plain program's by a relative error of at most 0.025.
Values may be sent and summed in bfloat16 or wider, within the bound.
A program may use at most 64 MiB of HBM per device.

v0:
```python
import jax
import jax.numpy as jnp
from jax import lax
from jax.sharding import PartitionSpec as P


def convolve(edge_cells, fresh_cells, kernel, edge_mask):
    sequence = jnp.concatenate(
        [edge_cells * edge_mask[:, :, None].astype(edge_cells.dtype), fresh_cells], 1
    ).astype(jnp.float32)
    steps_count = fresh_cells.shape[1]
    summed = kernel[0] * sequence[:, 0:steps_count]
    for offset in range(1, kernel.shape[0]):
        summed = summed + kernel[offset] * sequence[:, offset : offset + steps_count]
    return jax.nn.silu(summed).astype(jnp.bfloat16)


def shards(
    hidden_in,
    w_z,
    w_x,
    w_bc,
    w_dt,
    conv_x,
    conv_bc,
    dt_bias,
    a_log,
    d_skip,
    norm_gain,
    w_out,
    edge_x,
    edge_bc,
    pool,
    tenant_sizes,
    owner,
    accepted,
    prompt_len,
):
    highest = lax.Precision.HIGHEST
    rows_in = hidden_in[0]
    local_rows = rows_in.shape[0]
    n_req = edge_x.shape[0]
    drafts = local_rows * lax.axis_size("blk") // n_req
    state_dim = w_bc.shape[1] // 2
    heads_here = w_dt.shape[1]
    inner_here = w_z.shape[1]
    head_dim = inner_here // heads_here
    slots_here = pool.shape[0]
    cap_group = slots_here // lax.axis_size("rep")
    weights_in = (w_z, w_x, w_dt, w_bc)
    block_rows = lax.all_gather(rows_in, "blk", axis=0, tiled=True)
    projected = jnp.concatenate(
        [
            jnp.dot(block_rows, weight_cols, preferred_element_type=jnp.float32)
            for weight_cols in weights_in
        ],
        1,
    ).astype(jnp.bfloat16)
    z_all = projected[:, :inner_here]
    u_all = projected[:, inner_here : 2 * inner_here]
    dt_raw = projected[:, 2 * inner_here : 2 * inner_here + heads_here]
    bc_all = projected[:, 2 * inner_here + heads_here :]
    edge_len = edge_x.shape[1]
    edge_mask = prompt_len[:, None] >= (edge_len - jnp.arange(edge_len, dtype=jnp.int32))[None, :]
    x_conv = convolve(edge_x, u_all.reshape(n_req, drafts, inner_here), conv_x, edge_mask)
    bc_conv = convolve(edge_bc, bc_all.reshape(n_req, drafts, 2 * state_dim), conv_bc, edge_mask)
    b_half = bc_conv[:, :, :state_dim]
    c_half = bc_conv[:, :, state_dim:]
    b_float = b_half.astype(jnp.float32)
    c_float = c_half.astype(jnp.float32)
    x_heads = x_conv.reshape(n_req, drafts, heads_here, head_dim).astype(jnp.float32)
    req_index = lax.axis_index("rep") * n_req + jnp.arange(n_req, dtype=jnp.int32)
    tenant_ends = jnp.cumsum(tenant_sizes)
    tenant_id = jnp.sum((req_index[:, None] >= tenant_ends[None, :-1]).astype(jnp.int32), axis=1)
    tenant_pick = (
        tenant_id[:, None] == jnp.arange(tenant_sizes.shape[0], dtype=jnp.int32)[None, :]
    ).astype(jnp.float32)
    bias_req = jnp.dot(tenant_pick, dt_bias, precision=highest)
    step_size = jax.nn.softplus(
        dt_raw.reshape(n_req, drafts, heads_here).astype(jnp.float32) + bias_req[:, None, :]
    )
    log_decay = jnp.cumsum(step_size * (-jnp.exp(a_log))[None, None, :], axis=1)
    draft_index = jnp.arange(drafts, dtype=jnp.int32)
    causal = draft_index[:, None] >= draft_index[None, :]
    scores = jnp.einsum("rtn,rsn->rts", c_float, b_float, precision=highest)
    log_gap = log_decay[:, :, None, :] - log_decay[:, None, :, :]
    weight = (
        jnp.where(causal[None, :, :, None], jnp.exp(jnp.minimum(log_gap, 0.0)), 0.0)
        * step_size[:, None, :, :]
        * scores[:, :, :, None]
    )
    y_local = (
        jnp.einsum("rtsh,rshp->rthp", weight, x_heads, precision=highest)
        + d_skip[None, None, :, None] * x_heads
    )
    pick_last = (draft_index[None, :] == accepted[:, None] - 1).astype(jnp.float32)
    log_accept = jnp.sum(pick_last[:, :, None] * log_decay, axis=1)
    keep_draft = draft_index[None, :] < accepted[:, None]
    coef = (
        jnp.where(
            keep_draft[:, :, None],
            jnp.exp(jnp.minimum(log_accept[:, None, :] - log_decay, 0.0)),
            0.0,
        )
        * step_size
    )
    carry_decay = jnp.exp(log_accept)
    decay_now = jnp.exp(log_decay)
    owner_of = owner[:, 0]
    local_index = jnp.arange(n_req, dtype=jnp.int32)
    earlier = (owner_of[None, :] == owner_of[:, None]) & (
        local_index[None, :] < local_index[:, None]
    )
    rank_within = jnp.sum(earlier.astype(jnp.int32), axis=1)
    slot_index = owner_of * cap_group + rank_within
    fetched = lax.all_to_all(
        pool.astype(jnp.bfloat16), "rep", split_axis=0, concat_axis=0, tiled=True
    ).astype(pool.dtype)
    start_state = jnp.take(fetched, slot_index, axis=0)
    y_prior = decay_now[:, :, :, None] * jnp.einsum(
        "rhpn,rtn->rthp", start_state, c_float, precision=highest
    )
    accepted_state = carry_decay[:, :, None, None] * start_state + jnp.einsum(
        "rsh,rshp,rsn->rhpn", coef, x_heads, b_float, precision=highest
    )
    buffer = jnp.zeros(pool.shape, jnp.float32).at[slot_index].set(accepted_state)
    new_pool = lax.all_to_all(
        buffer.astype(jnp.bfloat16), "rep", split_axis=0, concat_axis=0, tiled=True
    ).astype(buffer.dtype)
    y_total = (y_local + y_prior).reshape(n_req * drafts, inner_here)
    gated = y_total * jax.nn.silu(z_all.astype(jnp.float32))
    sq_total = lax.psum(jnp.sum(gated * gated, axis=1), "blk")
    inner_all = inner_here * lax.axis_size("blk")
    normed = (gated * lax.rsqrt(sq_total / inner_all + 1e-05)[:, None] * norm_gain[None, :]).astype(
        jnp.bfloat16
    )
    block_rows = normed
    mixed = lax.psum_scatter(
        jnp.dot(block_rows, w_out, preferred_element_type=jnp.float32).astype(jnp.bfloat16),
        "blk",
        scatter_dimension=0,
        tiled=True,
    )
    return (mixed[None], new_pool)


def solution(mesh):
    placed = (
        P("rep", "blk", None),
        P(None, "blk"),
        P(None, "blk"),
        P(),
        P(None, "blk"),
        P(None, "blk"),
        P(),
        P(None, "blk"),
        P("blk"),
        P("blk"),
        P("blk"),
        P("blk", None),
        P("rep", None, "blk"),
        P("rep", None, None),
        P("rep", "blk", None, None),
        P(),
        P("rep", None),
        P("rep"),
        P("rep"),
    )
    return jax.shard_map(
        shards,
        mesh=mesh,
        in_specs=placed,
        out_specs=(P("rep", "blk", None), P("rep", "blk", None, None)),
        check_vma=False,
    )
```

profile of v0, /device:TPU:2, one launch (start us, length us, event | category | flops | bytes accessed | tf_op | source)
XLA Modules:
  0.0 418.3 jit_solution(11525417549869949106)
XLA Ops:
  7.2 0.0 copy-start
  7.2 0.0 all-gather.3.cloned.1.call-start
  7.2 0.7 all-gather.3.cloned.1.call-update
  7.9 3.4 convert_element_type.82
  11.4 5.9 %all-to-all-start = ((bf16[48,2,64,128]{3,2,1,0:T(8,128)(2,1)}), bf16[48,2,64,128]{3,2,1,0:T(8,128)(2,1)S(1)}, u32[]{:S(2)}, u32[]{:S(2)}) async-start(bf16[48,2,64,128]{3,2,1,0:T(8,128)(2,1)} %convert_element_type.82), calls=%async_computation | async-start | bytes 3145728 | tf_op jit(solution)/shard_map/all_to_all | solution.py:116
  17.3 0.2 reduce-window.4
  17.5 0.2 convert_reduce_fusion
  17.7 0.5 and_bitcast_fusion
  18.3 0.1 convert_reduce_fusion.1
  18.4 0.5 copy-done.10
  18.8 0.1 compare_convert_fusion
  18.9 0.1 broadcast_multiply_fusion
  19.0 0.6 iota_compare_fusion.5
  19.5 0.1 copy.81
  19.6 0.6 copy.75
  20.3 0.2 fusion.70
  20.4 0.6 slice_bitcast_fusion.4
  21.1 0.6 fusion.75
  21.7 0.6 fusion.72
  22.3 0.7 copy_multiply_fusion
  23.0 14.5 %all-to-all-done = bf16[48,2,64,128]{3,2,1,0:T(8,128)(2,1)S(1)} async-done(((bf16[48,2,64,128]{3,2,1,0:T(8,128)(2,1)}), bf16[48,2,64,128]{3,2,1,0:T(8,128)(2,1)S(1)}, u32[]{:S(2)}, u32[]{:S(2)}) %all-to-all-start) | async-done | bytes 1572896 | tf_op jit(solution)/shard_map/all_to_all | solution.py:116
  37.5 2.1 convert_element_type.83
  39.5 2.6 gather_fusion
  42.1 50.4 %all-gather.3.cloned.1.call-done = bf16[1,512,2560]{2,1,0:T(8,128)(2,1)} async-done(((bf16[1,16,2560]{2,1,0:T(8,128)(2,1)}), bf16[1,512,2560]{2,1,0:T(8,128)(2,1)}) %all-gather.3.cloned.1.call-update) | async-done | bytes 2621456 | tf_op jit(solution)/shard_map/all_gather | solution.py:51
  92.5 2.5 fusion.32
  95.0 0.1 reshape.171
  95.1 0.1 copy.76
  95.2 0.7 broadcast_multiply_fusion.1
  95.9 0.7 copy.80
  96.6 2.7 fusion.20
  99.3 0.1 maximum_convert_fusion.1
  99.4 0.2 multiply_convert_fusion.2
  99.6 0.9 reshape.167
  100.5 1.6 copy.77
  102.0 1.7 fusion.76
  103.7 1.2 copy.78
  104.9 1.7 multiply_reduce_fusion
  106.7 1.2 copy.85
  107.9 2.6 fusion.17
  110.6 0.1 maximum_convert_fusion
  110.7 0.3 multiply_convert_fusion
  111.1 0.2 fusion.65
  111.3 0.2 copy-done.3
  111.5 0.6 fusion.16
  112.1 2.6 fusion.13
  114.8 1.1 copy.86
  115.8 2.0 reshape.170
  117.9 1.8 copy.87
  119.7 3.7 multiply_reduce_fusion.1
  123.4 72.2 %psum.7 = f32[512]{0:T(512)S(1)} all-reduce(f32[512]{0:T(512)S(1)} %get-tuple-element.16), channel_id=1, replica_groups=mesh['blk'=32,'rep'=8] {'blk'}, use_global_device_ids=true, to_apply=%region_5.6 | all-reduce | flops 512 | bytes 4096 | tf_op jit(solution)/shard_map/psum | solution.py:132
  195.6 3.6 convolution_convert_fusion
  199.2 0.0 reduce-scatter.2.cloned.1.call-update
  199.2 0.6 copy-done.26
  199.9 1.1 copy.89
  201.0 0.1 copy.88
  201.1 0.1 copy.90
  201.2 4.6 %multiply_add_fusion = f32[32,2,64,128]{3,2,1,0:T(8,128)} fusion(f32[32,2,64,128]{3,2,1,0:T(8,128)S(1)} %gather_fusion, f32[32,2]{1,0:T(8,128)S(1)} %exp.50, pred[32]{0:T(512)(128)(4,1)S(1)} %copy-done.12, f32[32,16,2]{1,2,0:T(2,128)S(1)} %copy.90, bf16[32,16,2,64]{3,2,1,0:T(2,128)(2,1)} %reshape.167, bf16[32,16,256]{2,1,0:T(8,128)(2,1)} %copy-done.2), kind=kOutput, calls=%fused_computation.11 | convolution fusion | flops 102367232 | bytes 4591904 | tf_op jit(solution)/shard_map/rsh,rshp,rsn->rhpn/dot_general | solution.py:123
  205.7 2.1 broadcast_in_dim.31
  207.8 0.1 copy-done.1
  207.9 5.3 %scatter_fusion = f32[48,2,64,128]{3,2,1,0:T(8,128)} fusion(f32[48,2,64,128]{3,2,1,0:T(8,128)} %broadcast_in_dim.31, s32[32]{0:T(128)S(1)} %bitcast.79, f32[32,2,64,128]{3,2,1,0:T(8,128)S(1)} %copy-done.1), kind=kCustom, calls=%fused_computation.1 | custom fusion | bytes 6291584 | tf_op jit(solution)/shard_map/scatter | solution.py:126
  213.2 2.3 convert_element_type.88
  215.5 24.9 %all_to_all.10 = bf16[48,2,64,128]{3,2,1,0:T(8,128)(2,1)S(1)} all-to-all(bf16[48,2,64,128]{3,2,1,0:T(8,128)(2,1)S(1)} %convert_element_type.88), channel_id=1, replica_groups=mesh['blk'=32,'rep'=8] {'rep'}, dimensions={0} | all-to-all | bytes 3145728 | tf_op jit(solution)/shard_map/all_to_all | solution.py:127
  240.4 2.0 convert_element_type.89
  242.5 169.0 %reduce-scatter.2.cloned.1.call-done = bf16[16,2560]{1,0:T(8,128)(2,1)} async-done(((bf16[512,2560]{1,0:T(8,128)(2,1)}), bf16[16,2560]{1,0:T(8,128)(2,1)}) %reduce-scatter.2.cloned.1.call-update) | async-done | bytes 81936 | tf_op jit(solution)/shard_map/reduce_scatter | solution.py:138
  (72 shorter events, 0.2 us)
Async XLA Ops:
  7.2 100.7 %copy-start = (bf16[2560,256]{1,0:T(8,128)(2,1)S(1)}, bf16[2560,256]{1,0:T(8,128)(2,1)}, u32[]{:S(2)}) copy-start(bf16[2560,256]{1,0:T(8,128)(2,1)} %param.22) | copy-start | bytes 3932164
  7.2 85.3 %all-gather.3.cloned.1.call-start = ((), (), s32[]{:S(2)}) async-start(), calls=%async_computation.4 | async-start | bytes 2703360 | tf_op jit(solution)/shard_map/all_gather | solution.py:51
  11.3 6.0 %copy-start.30 = (s32[4]{0:T(128)S(1)}, s32[4]{0:T(128)}, u32[]{:S(2)}) copy-start(s32[4]{0:T(128)} %param.34) | copy-start | bytes 52
  11.3 6.2 %copy-start.27 = (s32[32,1]{0,1:T(1,128)S(1)}, s32[32,1]{0,1:T(1,128)}, u32[]{:S(2)}) copy-start(s32[32,1]{0,1:T(1,128)} %param.35) | copy-start | bytes 388
  11.3 7.0 %copy-start.31 = (f32[2]{0:T(128)S(1)}, f32[2]{0:T(128)}, u32[]{:S(2)}) copy-start(f32[2]{0:T(128)} %param.27) | copy-start | bytes 28
  11.3 7.5 %copy-start.28 = (s32[32]{0:T(128)S(1)}, s32[32]{0:T(128)}, u32[]{:S(2)}) copy-start(s32[32]{0:T(128)} %param.37) | copy-start | bytes 388
  11.3 7.5 %copy-start.8 = (bf16[32,3,128]{2,0,1:T(8,128)(2,1)S(1)}, bf16[32,3,128]{2,0,1:T(8,128)(2,1)}, u32[]{:S(2)}) copy-start(bf16[32,3,128]{2,0,1:T(8,128)(2,1)} %param.31) | copy-start | bytes 73732
  11.4 8.9 %copy-start.25 = (s32[32]{0:T(128)S(1)}, s32[32]{0:T(128)}, u32[]{:S(2)}) copy-start(s32[32]{0:T(128)} %param.36) | copy-start | bytes 388
  11.4 8.9 %copy-start.29 = (f32[4,2]{0,1:T(2,128)S(1)}, f32[4,2]{0,1:T(2,128)}, u32[]{:S(2)}) copy-start(f32[4,2]{0,1:T(2,128)} %param.26) | copy-start | bytes 100
  11.4 9.1 %copy-start.22 = (f32[4,128]{1,0:T(4,128)S(1)}, f32[4,128]{1,0:T(4,128)}, u32[]{:S(2)}) copy-start(f32[4,128]{1,0:T(4,128)} %param.24) | copy-start | bytes 6148
  11.4 9.7 %copy-start.17 = (f32[4,256]{1,0:T(4,128)S(1)}, f32[4,256]{1,0:T(4,128)}, u32[]{:S(2)}) copy-start(f32[4,256]{1,0:T(4,128)} %param.25) | copy-start | bytes 12292
  11.4 10.8 %copy-start.6 = (bf16[32,3,256]{2,0,1:T(8,128)(2,1)S(1)}, bf16[32,3,256]{2,0,1:T(8,128)(2,1)}, u32[]{:S(2)}) copy-start(bf16[32,3,256]{2,0,1:T(8,128)(2,1)} %param.32) | copy-start | bytes 147460
  11.4 26.1 %all-to-all-start = ((bf16[48,2,64,128]{3,2,1,0:T(8,128)(2,1)}), bf16[48,2,64,128]{3,2,1,0:T(8,128)(2,1)S(1)}, u32[]{:S(2)}, u32[]{:S(2)}) async-start(bf16[48,2,64,128]{3,2,1,0:T(8,128)(2,1)} %convert_element_type.82), calls=%async_computation | async-start | bytes 3145728 | tf_op jit(solution)/shard_map/all_to_all | solution.py:116
  17.3 394.1 %reduce-scatter.2.cloned.1.call-start = ((), (), s32[]{:S(2)}) async-start(), calls=%async_computation.3 | async-start | bytes 2703360 | tf_op jit(solution)/shard_map/reduce_scatter | solution.py:138
  18.2 0.6 copy-start.10
  39.5 53.0 %copy-start.9 = (bf16[2560,2]{0,1:T(2,128)(2,1)S(1)}, bf16[2560,2]{0,1:T(2,128)(2,1)}, u32[]{:S(2)}) copy-start(bf16[2560,2]{0,1:T(2,128)(2,1)} %param.23) | copy-start | bytes 30724
  96.6 2.8 copy-start.5
  96.6 2.8 copy-start.18
  96.6 2.8 copy-start.19
  96.6 2.8 copy-start.20
  96.6 2.8 copy-start.21
  107.9 2.7 copy-start.4
  107.9 2.8 copy-start.13
  107.9 2.8 copy-start.14
  107.9 2.8 copy-start.15
  107.9 2.8 copy-start.16
  110.5 1.0 copy-start.3
  110.5 0.9 copy-start.7
  110.6 0.9 copy-start.23
  110.6 0.9 copy-start.32
  110.7 1.4 copy-start.12
  111.1 3.7 copy-start.2
  119.7 75.9 %copy-start.24 = (f32[128]{0:T(128)S(1)}, f32[128]{0:T(128)}, u32[]{:S(2)}) copy-start(f32[128]{0:T(128)} %param.29) | copy-start | bytes 1540
  199.2 0.7 copy-start.26
  205.7 2.1 copy-start.1
  205.7 2.1 copy-start.11
Sparse Core Ops, SparseCore 0:
  10.6 81.8 all-gather.2
  199.3 212.0 reduce-scatter.1
where the time goes:
time: 419 us; the launch traced here: 418 us
  waiting for transfers between devices  235 us (56%)
  blocking collectives  97.1 us (23%)
  local copies, waits for them, and re-layouts  25.3 us (6%)
  matrix products  23.3 us (6%)
  other arithmetic  17.6 us (4%)
  between operations  14.4 us (3%)
  starting transfers between devices  5.94 us (1%)
    reduce_scatter x1, waiting for transfers between devices, shards(): lax.psum_scatter(jnp.dot(block_rows, w_out, preferred_element_type=jnp.fl...  169 us
    psum x1, blocking collectives, shards(): sq_total = lax.psum(jnp.sum(gated * gated, axis=1), 'blk')  72.2 us
    all_gather x1, waiting for transfers between devices, shards(): block_rows = lax.all_gather(rows_in, 'blk', axis=0, tiled=True)  50.4 us
    all_to_all x1, blocking collectives, shards(): lax.all_to_all(buffer.astype(jnp.bfloat16), 'rep', split_axis=0, concat_a...  24.9 us
    all_to_all x1, waiting for transfers between devices, shards(): lax.all_to_all(pool.astype(jnp.bfloat16), 'rep', split_axis=0, concat_axi...  14.5 us
    dot_general x4, matrix products, shards(): jnp.dot(block_rows, weight_cols, preferred_element_type=jnp.float32)  11.5 us
  transfers between devices with their start and end apart: 3, of which 3 were waited for; matrix products, arithmetic and copies ran while one was open for 7% of the time, Pallas kernels for 0%

commit v1 on v0

--- a/solution.py
+++ b/solution.py
@@ -129,7 +129,7 @@
     ).astype(buffer.dtype)
     y_total = (y_local + y_prior).reshape(n_req * drafts, inner_here)
     gated = y_total * jax.nn.silu(z_all.astype(jnp.float32))
-    sq_total = lax.psum(jnp.sum(gated * gated, axis=1), "blk")
+    sq_total = jnp.sum(lax.all_gather(jnp.sum(gated * gated, axis=1), "blk"), axis=0)
     inner_all = inner_here * lax.axis_size("blk")
     normed = (gated * lax.rsqrt(sq_total / inner_all + 1e-05)[:, None] * norm_gain[None, :]).astype(
         jnp.bfloat16

time: 419 us -> 399 us (0.952)
  blocking collectives: 97.1 us -> 72.2 us
    psum x1 -> x0, blocking collectives: 72.2 us -> none  [shards(): sq_total = lax.psum(jnp.sum(gated * gated, axis=1), 'blk')]
    all_gather x0 -> x1, blocking collectives: none -> 47.3 us  [shards(): lax.all_gather(jnp.sum(gated * gated, axis=1), 'blk')]
  transfers between devices with their start and end apart: 3 -> 3, of which waited for: 3 -> 3; matrix products, arithmetic and copies ran while one was open for 7% -> 8% of each run, Pallas kernels for 0% -> 0%
where the time goes in v1:
time: 399 us; the launch traced here: 398 us
  waiting for transfers between devices  239 us (60%)
  blocking collectives  72.2 us (18%)
  local copies, waits for them, and re-layouts  25.4 us (6%)
  matrix products  23.3 us (6%)
  other arithmetic  17.7 us (4%)
  between operations  14.4 us (4%)
  starting transfers between devices  5.94 us (1%)
    reduce_scatter x1, waiting for transfers between devices, shards(): lax.psum_scatter(jnp.dot(block_rows, w_out, preferred_element_type=jnp.fl...  173 us
    all_gather x1, waiting for transfers between devices, shards(): block_rows = lax.all_gather(rows_in, 'blk', axis=0, tiled=True)  50.4 us
    all_gather x1, blocking collectives, shards(): lax.all_gather(jnp.sum(gated * gated, axis=1), 'blk')  47.3 us
    all_to_all x1, blocking collectives, shards(): lax.all_to_all(buffer.astype(jnp.bfloat16), 'rep', split_axis=0, concat_a...  25 us
    all_to_all x1, waiting for transfers between devices, shards(): lax.all_to_all(pool.astype(jnp.bfloat16), 'rep', split_axis=0, concat_axi...  14.5 us
    dot_general x4, matrix products, shards(): jnp.dot(block_rows, weight_cols, preferred_element_type=jnp.float32)  11.5 us
  transfers between devices with their start and end apart: 3, of which 3 were waited for; matrix products, arithmetic and copies ran while one was open for 8% of the time, Pallas kernels for 0%

profile of v1, /device:TPU:2, one launch (start us, length us, event | category | flops | bytes accessed | tf_op | source)
XLA Modules:
  0.0 397.6 jit_solution(3180963296703493404)
XLA Ops:
  7.2 0.0 all-gather.5.cloned.1.call-start
  7.2 0.7 all-gather.5.cloned.1.call-update
  7.9 3.4 convert_element_type.82
  11.4 5.9 %all-to-all-start = ((bf16[48,2,64,128]{3,2,1,0:T(8,128)(2,1)}), bf16[48,2,64,128]{3,2,1,0:T(8,128)(2,1)S(1)}, u32[]{:S(2)}, u32[]{:S(2)}) async-start(bf16[48,2,64,128]{3,2,1,0:T(8,128)(2,1)} %convert_element_type.82), calls=%async_computation | async-start | bytes 3145728 | tf_op jit(solution)/shard_map/all_to_all | solution.py:116
  17.3 0.2 reduce-window.4
  17.5 0.2 convert_reduce_fusion
  17.7 0.5 and_bitcast_fusion
  18.3 0.1 convert_reduce_fusion.1
  18.4 0.5 copy-done.10
  18.8 0.1 compare_convert_fusion
  18.9 0.1 broadcast_multiply_fusion
  19.0 0.6 iota_compare_fusion.5
  19.5 0.1 copy.95
  19.6 0.6 copy.89
  20.3 0.2 fusion.70
  20.4 0.6 slice_bitcast_fusion.4
  21.1 0.6 fusion.75
  21.7 0.6 fusion.72
  22.3 0.7 copy_multiply_fusion
  23.0 14.5 %all-to-all-done = bf16[48,2,64,128]{3,2,1,0:T(8,128)(2,1)S(1)} async-done(((bf16[48,2,64,128]{3,2,1,0:T(8,128)(2,1)}), bf16[48,2,64,128]{3,2,1,0:T(8,128)(2,1)S(1)}, u32[]{:S(2)}, u32[]{:S(2)}) %all-to-all-start) | async-done | bytes 1572896 | tf_op jit(solution)/shard_map/all_to_all | solution.py:116
  37.5 2.1 convert_element_type.83
  39.5 2.6 gather_fusion
  42.1 50.4 %all-gather.5.cloned.1.call-done = bf16[1,512,2560]{2,1,0:T(8,128)(2,1)} async-done(((bf16[1,16,2560]{2,1,0:T(8,128)(2,1)}), bf16[1,512,2560]{2,1,0:T(8,128)(2,1)}) %all-gather.5.cloned.1.call-update) | async-done | bytes 2621456 | tf_op jit(solution)/shard_map/all_gather | solution.py:51
  92.5 2.5 fusion.32
  95.0 0.1 reshape.175
  95.1 0.1 copy.90
  95.2 0.7 broadcast_multiply_fusion.1
  95.9 0.7 copy.94
  96.6 2.7 fusion.20
  99.3 0.1 maximum_convert_fusion.1
  99.4 0.2 multiply_convert_fusion.2
  99.6 0.9 reshape.171
  100.5 1.6 copy.91
  102.0 1.7 fusion.76
  103.7 1.2 copy.92
  104.9 1.7 multiply_reduce_fusion
  106.7 1.2 copy.99
  107.9 2.6 fusion.17
  110.6 0.1 maximum_convert_fusion
  110.7 0.3 multiply_convert_fusion
  111.1 0.2 fusion.65
  111.3 0.2 copy-done.3
  111.5 0.6 fusion.16
  112.1 2.6 fusion.13
  114.8 1.1 copy.100
  115.8 2.0 reshape.174
  117.9 1.8 copy.101
  119.7 3.7 multiply_reduce_fusion.1
  123.4 47.3 %all-gather.2 = f32[32,1,512]{2,1,0:T(1,128)S(1)} all-gather(f32[1,1,512]{2,1,0:T(1,128)S(1)} %bitcast.85), channel_id=3, replica_groups=mesh['blk'=32,'rep'=8] {'blk'}, dimensions={0}, use_global_device_ids=true | all-gather | bytes 67584 | tf_op jit(solution)/shard_map/all_gather | solution.py:132
  170.6 0.1 reduce_sum.51
  170.7 3.6 convolution_convert_fusion
  174.3 0.0 reduce-scatter.2.cloned.1.call-update
  174.4 0.6 copy-done.26
  175.0 1.1 copy.103
  176.1 0.1 copy.102
  176.2 0.1 copy.104
  176.3 4.6 %multiply_add_fusion = f32[32,2,64,128]{3,2,1,0:T(8,128)} fusion(f32[32,2,64,128]{3,2,1,0:T(8,128)S(1)} %gather_fusion, f32[32,2]{1,0:T(8,128)S(1)} %exp.50, pred[32]{0:T(512)(128)(4,1)S(1)} %copy-done.12, f32[32,16,2]{1,2,0:T(2,128)S(1)} %copy.104, bf16[32,16,2,64]{3,2,1,0:T(2,128)(2,1)} %reshape.171, bf16[32,16,256]{2,1,0:T(8,128)(2,1)} %copy-done.2), kind=kOutput, calls=%fused_computation.11 | convolution fusion | flops 102367232 | bytes 4591904 | tf_op jit(solution)/shard_map/rsh,rshp,rsn->rhpn/dot_general | solution.py:123
  180.9 2.1 broadcast_in_dim.31
  182.9 0.1 copy-done.1
  183.0 5.4 %scatter_fusion = f32[48,2,64,128]{3,2,1,0:T(8,128)} fusion(f32[48,2,64,128]{3,2,1,0:T(8,128)} %broadcast_in_dim.31, s32[32]{0:T(128)S(1)} %bitcast.80, f32[32,2,64,128]{3,2,1,0:T(8,128)S(1)} %copy-done.1), kind=kCustom, calls=%fused_computation.1 | custom fusion | bytes 6291584 | tf_op jit(solution)/shard_map/scatter | solution.py:126
  188.4 2.3 convert_element_type.88
  190.7 25.0 %all_to_all.10 = bf16[48,2,64,128]{3,2,1,0:T(8,128)(2,1)S(1)} all-to-all(bf16[48,2,64,128]{3,2,1,0:T(8,128)(2,1)S(1)} %convert_element_type.88), channel_id=1, replica_groups=mesh['blk'=32,'rep'=8] {'rep'}, dimensions={0} | all-to-all | bytes 3145728 | tf_op jit(solution)/shard_map/all_to_all | solution.py:127
  215.6 2.0 convert_element_type.89
  217.7 173.1 %reduce-scatter.2.cloned.1.call-done = bf16[16,2560]{1,0:T(8,128)(2,1)} async-done(((bf16[512,2560]{1,0:T(8,128)(2,1)}), bf16[16,2560]{1,0:T(8,128)(2,1)}) %reduce-scatter.2.cloned.1.call-update) | async-done | bytes 81936 | tf_op jit(solution)/shard_map/reduce_scatter | solution.py:138
  (73 shorter events, 0.2 us)
Async XLA Ops:
  7.2 100.7 %copy-start = (bf16[2560,256]{1,0:T(8,128)(2,1)S(1)}, bf16[2560,256]{1,0:T(8,128)(2,1)}, u32[]{:S(2)}) copy-start(bf16[2560,256]{1,0:T(8,128)(2,1)} %param.22) | copy-start | bytes 3932164
  7.2 85.3 %all-gather.5.cloned.1.call-start = ((), (), s32[]{:S(2)}) async-start(), calls=%async_computation.4 | async-start | bytes 2703360 | tf_op jit(solution)/shard_map/all_gather | solution.py:51
  11.3 6.0 %copy-start.30 = (s32[4]{0:T(128)S(1)}, s32[4]{0:T(128)}, u32[]{:S(2)}) copy-start(s32[4]{0:T(128)} %param.34) | copy-start | bytes 52
  11.3 6.2 %copy-start.27 = (s32[32,1]{0,1:T(1,128)S(1)}, s32[32,1]{0,1:T(1,128)}, u32[]{:S(2)}) copy-start(s32[32,1]{0,1:T(1,128)} %param.35) | copy-start | bytes 388
  11.3 7.0 %copy-start.31 = (f32[2]{0:T(128)S(1)}, f32[2]{0:T(128)}, u32[]{:S(2)}) copy-start(f32[2]{0:T(128)} %param.27) | copy-start | bytes 28
  11.3 7.5 %copy-start.28 = (s32[32]{0:T(128)S(1)}, s32[32]{0:T(128)}, u32[]{:S(2)}) copy-start(s32[32]{0:T(128)} %param.37) | copy-start | bytes 388
  11.3 7.5 %copy-start.8 = (bf16[32,3,128]{2,0,1:T(8,128)(2,1)S(1)}, bf16[32,3,128]{2,0,1:T(8,128)(2,1)}, u32[]{:S(2)}) copy-start(bf16[32,3,128]{2,0,1:T(8,128)(2,1)} %param.31) | copy-start | bytes 73732
  11.4 8.9 %copy-start.25 = (s32[32]{0:T(128)S(1)}, s32[32]{0:T(128)}, u32[]{:S(2)}) copy-start(s32[32]{0:T(128)} %param.36) | copy-start | bytes 388
  11.4 8.9 %copy-start.29 = (f32[4,2]{0,1:T(2,128)S(1)}, f32[4,2]{0,1:T(2,128)}, u32[]{:S(2)}) copy-start(f32[4,2]{0,1:T(2,128)} %param.26) | copy-start | bytes 100
  11.4 9.1 %copy-start.22 = (f32[4,128]{1,0:T(4,128)S(1)}, f32[4,128]{1,0:T(4,128)}, u32[]{:S(2)}) copy-start(f32[4,128]{1,0:T(4,128)} %param.24) | copy-start | bytes 6148
  11.4 9.7 %copy-start.17 = (f32[4,256]{1,0:T(4,128)S(1)}, f32[4,256]{1,0:T(4,128)}, u32[]{:S(2)}) copy-start(f32[4,256]{1,0:T(4,128)} %param.25) | copy-start | bytes 12292
  11.4 10.8 %copy-start.6 = (bf16[32,3,256]{2,0,1:T(8,128)(2,1)S(1)}, bf16[32,3,256]{2,0,1:T(8,128)(2,1)}, u32[]{:S(2)}) copy-start(bf16[32,3,256]{2,0,1:T(8,128)(2,1)} %param.32) | copy-start | bytes 147460
  11.4 26.1 %all-to-all-start = ((bf16[48,2,64,128]{3,2,1,0:T(8,128)(2,1)}), bf16[48,2,64,128]{3,2,1,0:T(8,128)(2,1)S(1)}, u32[]{:S(2)}, u32[]{:S(2)}) async-start(bf16[48,2,64,128]{3,2,1,0:T(8,128)(2,1)} %convert_element_type.82), calls=%async_computation | async-start | bytes 3145728 | tf_op jit(solution)/shard_map/all_to_all | solution.py:116
  17.3 373.5 %reduce-scatter.2.cloned.1.call-start = ((), (), s32[]{:S(2)}) async-start(), calls=%async_computation.3 | async-start | bytes 2703360 | tf_op jit(solution)/shard_map/reduce_scatter | solution.py:138
  18.2 0.6 copy-start.10
  39.5 53.0 %copy-start.9 = (bf16[2560,2]{0,1:T(2,128)(2,1)S(1)}, bf16[2560,2]{0,1:T(2,128)(2,1)}, u32[]{:S(2)}) copy-start(bf16[2560,2]{0,1:T(2,128)(2,1)} %param.23) | copy-start | bytes 30724
  96.6 2.8 copy-start.5
  96.6 2.8 copy-start.18
  96.6 2.8 copy-start.19
  96.6 2.8 copy-start.20
  96.6 2.8 copy-start.21
  107.9 2.7 copy-start.4
  107.9 2.8 copy-start.13
  107.9 2.8 copy-start.14
  107.9 2.8 copy-start.15
  107.9 2.8 copy-start.16
  110.5 1.0 copy-start.3
  110.5 0.9 copy-start.7
  110.6 0.9 copy-start.23
  110.6 0.9 copy-start.32
  110.7 1.4 copy-start.12
  111.1 3.7 copy-start.2
  119.7 51.1 %copy-start.24 = (f32[128]{0:T(128)S(1)}, f32[128]{0:T(128)}, u32[]{:S(2)}) copy-start(f32[128]{0:T(128)} %param.29) | copy-start | bytes 1540
  174.3 0.7 copy-start.26
  180.9 2.1 copy-start.1
  180.9 2.1 copy-start.11
Sparse Core Ops, SparseCore 0:
  10.6 81.8 all-gather.4
  174.5 216.2 reduce-scatter.1
